TPU v7x, 32 devices: a whole 2x2x4 slice. The times are simulated.
32 devices in a mesh: fsdp: 8 (over y, x, core), group: 4 (over z).
Axes of the slice: x: 2, y: 2, z: 4, core: 2. Of those that a mesh axis runs over, the one named last changes fastest.
Arguments:
- gradient: bfloat16 [4, 512, 4096], P('group', 'fsdp'), may hold values from -4000 to 4000
- first_moment: bfloat16 [4, 4096, 512], P('group', 'fsdp'), may hold values from -3 to 3
- second_moment: bfloat16 [4, 4096, 512], P('group', 'fsdp'), may hold values from 0.29882812 to 3
- basis_store: bfloat16 [4, 4608, 256], P('group', 'fsdp'), may hold values from -1 to 2
- step_number: int32 [1], replicated, may hold values from 1 to 99999
- matrix_ids: int32 [4], P('group'), may hold values from 0 to 3, each once
Outputs:
- update: bfloat16 [4, 512, 4096], P('group', 'fsdp')
- new_first: bfloat16 [4, 4096, 512], P('group', 'fsdp')
- new_second: bfloat16 [4, 4096, 512], P('group', 'fsdp')
Inputs may be any that keep to these rules, and one draw needn't show every extreme that they name: `matrix_ids`: each matrix index once.
All inputs are finite; a program needn't handle non-finite values.
Results may differ from a plain program's by a relative error of at most 0.0004.
Values may be sent and summed in bfloat16 or wider, within the bound.
A program may use at most 64 MiB of HBM per device.

v0:
```python
import math
import jax
import jax.numpy as jnp
from jax import lax
from jax.sharding import PartitionSpec as P

BLOCK = 256
BETA_ONE = 0.95
BETA_TWO = 0.95
ADAM_EPS = 1e-08
HIGHEST = lax.Precision.HIGHEST


def clip_of(local_squares, entries):
    total = lax.psum(local_squares, ("fsdp", "group"))
    return jnp.float32(math.sqrt(entries)) / (jnp.sqrt(total) + 1e-06)


def local(gradient, first_moment, second_moment, basis_store, step_number, matrix_ids):
    fsdp_count = lax.axis_size("fsdp")
    group_count = lax.axis_size("group")
    row_count = gradient.shape[1]
    col_count = gradient.shape[2]
    all_rows = row_count * fsdp_count
    col_share = col_count // fsdp_count
    left_blocks = all_rows // BLOCK
    right_blocks = col_count // BLOCK
    entries = all_rows * col_count * group_count
    grad_local = gradient[0].astype(jnp.float32)
    local_squares = jnp.sum(grad_local * grad_local)
    gathered = lax.all_gather(basis_store[0], "fsdp", axis=0, tiled=True)
    owner_rows = basis_store.shape[1]
    owner = (step_number[0] + matrix_ids[0]) % fsdp_count
    ordered_half = jnp.roll(gathered, -owner * owner_rows, axis=0)
    left = ordered_half[:all_rows].astype(jnp.float32).reshape(left_blocks, BLOCK, BLOCK)
    right_half = ordered_half[all_rows:].reshape(right_blocks, BLOCK, BLOCK)
    right = right_half.astype(jnp.float32)
    turned = jnp.einsum(
        "rbj,bjl->rbl",
        gradient[0].reshape(row_count, right_blocks, BLOCK),
        right_half,
        preferred_element_type=jnp.float32,
    )
    turned = clip_of(local_squares, entries) * turned
    outgoing = turned.reshape(row_count, fsdp_count, col_share)
    received = lax.all_to_all(outgoing, "fsdp", split_axis=1, concat_axis=0, tiled=True)
    width = received.shape[2]
    columns = received[:, 0, :].reshape(left_blocks, BLOCK, width)
    rotated = jnp.einsum("bkc,bki->cbi", columns, left, precision=HIGHEST).reshape(width, all_rows)
    count = step_number[0].astype(jnp.float32)
    first_fix = 1.0 - jnp.power(jnp.float32(BETA_ONE), count)
    second_fix = 1.0 - jnp.power(jnp.float32(BETA_TWO), count)
    first_sum = BETA_ONE * first_moment[0].astype(jnp.float32) + (1.0 - BETA_ONE) * rotated
    second_sum = (
        BETA_TWO * second_moment[0].astype(jnp.float32) + (1.0 - BETA_TWO) * rotated * rotated
    )
    direction = first_sum / first_fix / (jnp.sqrt(second_sum / second_fix) + ADAM_EPS)
    backward = jnp.einsum(
        "cbi,bki->cbk", direction.reshape(col_share, left_blocks, BLOCK), left, precision=HIGHEST
    )
    returning = backward.reshape(col_share, fsdp_count, row_count)
    received = lax.all_to_all(returning, "fsdp", split_axis=1, concat_axis=0, tiled=True)
    width = received.shape[2]
    pieces = received[:, 0, :].reshape(right_blocks, BLOCK, width)
    result = jnp.einsum("blr,bjl->rbj", pieces, right, precision=HIGHEST).reshape(width, col_count)
    return (
        result[None].astype(jnp.bfloat16),
        first_sum[None].astype(jnp.bfloat16),
        second_sum[None].astype(jnp.bfloat16),
    )


def solution(mesh):
    in_specs = (
        P("group", "fsdp", None),
        P("group", "fsdp", None),
        P("group", "fsdp", None),
        P("group", "fsdp", None),
        P(),
        P("group"),
    )
    out_specs = (P("group", "fsdp", None), P("group", "fsdp", None), P("group", "fsdp", None))
    return jax.shard_map(local, mesh=mesh, in_specs=in_specs, out_specs=out_specs, check_vma=False)
```

profile of v0, /device:TPU:0, one launch (start us, length us, event | category | flops | bytes accessed | tf_op | source)
XLA Modules:
  0.0 129.9 jit_solution(4664834779437250794)
XLA Ops:
  7.2 0.0 all-gather.3.cloned.1.call-start
  7.2 0.7 all-gather.3.cloned.1.call-update
  7.9 1.9 %multiply_reduce_fusion = f32[]{:T(128)} fusion(bf16[1,64,4096]{2,1,0:T(8,128)(2,1)} %param.6), kind=kLoop, calls=%fused_computation.24 | loop fusion | flops 786431 | bytes 524292 | tf_op jit(solution)/shard_map/reduce_sum | solution.py:30
  9.8 42.2 %psum.7 = f32[]{:T(128)} all-reduce(f32[]{:T(128)} %multiply_reduce_fusion), channel_id=1, replica_groups=mesh['fsdp'=8,'group'=4] {'fsdp','group'}, use_global_device_ids=true, to_apply=%region_1.2 | all-reduce | flops 1 | bytes 8 | tf_op jit(solution)/shard_map/psum | solution.py:15
  54.0 1.1 copy.42
  55.2 0.0 all-gather.3.cloned.1.call-done
  55.3 3.7 %fusion = bf16[4608,256]{1,0:T(8,128)(2,1)S(1)} fusion(s32[]{:T(128)S(6)} %select_n.21, bf16[4608,256]{1,0:T(8,128)(2,1)} %bitcast.46), kind=kLoop, calls=%fused_computation.2 | loop fusion | flops 4718592 | bytes 4718596 | tf_op jit(solution)/shard_map/jit(_roll_dynamic)/concatenate | solution.py:34
  59.0 0.0 copy-start
  59.0 0.1 slice.8
  59.2 0.5 fusion.1
  59.6 0.8 copy-done
  60.4 0.6 copy.30
  61.0 1.3 %reshape.80 = f32[64,8,512]{2,1,0:T(8,128)} reshape(f32[64,16,256]{2,1,0:T(8,128)S(1)} %copy.30) | data formatting | bytes 2097152 | tf_op jit(solution)/shard_map/reshape | solution.py:45
  62.3 2.8 %copy.31 = f32[64,8,512]{2,0,1:T(8,128)} copy(f32[64,8,512]{2,1,0:T(8,128)} %reshape.80) | data formatting | bytes 2097152 | tf_op jit(solution)/shard_map/reshape | solution.py:45
  65.1 3.8 %all-to-all-start = ((f32[64,8,512]{2,0,1:T(8,128)}), f32[64,8,512]{2,0,1:T(8,128)S(1)}, u32[]{:S(2)}, u32[]{:S(2)}) async-start(f32[64,8,512]{2,0,1:T(8,128)} %copy.31), calls=%async_computation | async-start | bytes 2097152 | tf_op jit(solution)/shard_map/all_to_all | solution.py:46
  69.0 1.0 slice.9
  69.9 14.4 %all-to-all-done = f32[64,8,512]{2,0,1:T(8,128)S(1)} async-done(((f32[64,8,512]{2,0,1:T(8,128)}), f32[64,8,512]{2,0,1:T(8,128)S(1)}, u32[]{:S(2)}, u32[]{:S(2)}) %all-to-all-start) | async-done | bytes 1048608 | tf_op jit(solution)/shard_map/all_to_all | solution.py:46
  84.3 1.7 %fusion.23 = f32[2,256,512]{2,1,0:T(8,128)} fusion(bf16[2,256,256]{2,1,0:T(8,128)(2,1)S(1)} %bitcast.49, f32[2,256,512]{2,1,0:T(8,128)S(1)} %bitcast.43), kind=kOutput, calls=%fused_computation.32 | convolution fusion | flops 805306368 | bytes 2359296 | tf_op jit(solution)/shard_map/bkc,bki->cbi/dot_general | solution.py:49
  86.0 2.5 %copy.38 = f32[1,512,512]{2,1,0:T(8,128)} copy(f32[1,512,512]{1,2,0:T(8,128)} %bitcast.44) | data formatting | bytes 2097152 | tf_op jit(solution)/shard_map/reshape | solution.py:49
  88.6 3.0 %fusion.14 = (bf16[1,512,512]{2,1,0:T(8,128)(2,1)}, bf16[1,512,512]{2,1,0:T(8,128)(2,1)}, f32[1,512,512]{2,1,0:T(8,128)}, f32[1,512,512]{2,1,0:T(8,128)S(1)}) fusion(f32[1,512,512]{2,1,0:T(8,128)} %copy.38, bf16[1,512,512]{2,1,0:T(8,128)(2,1)} %param.8, bf16[1,512,512]{2,1,0:T(8,128)(2,1)} %param.7), kind=kLoop, calls=%fused_computation.20 | loop fusion | flops 2621440 | bytes 5242880 | tf_op jit(solution)/shard_map/convert_element_type | solution.py:69
  91.6 2.6 %copy.28 = f32[1,512,512]{1,2,0:T(8,128)} copy(f32[1,512,512]{2,1,0:T(8,128)} %get-tuple-element.5) | data formatting | bytes 2097152 | tf_op jit(solution)/shard_map/mul | solution.py:53
  94.2 1.3 %copy.33 = f32[1,512,512]{1,2,0:T(8,128)} copy(f32[1,512,512]{2,1,0:T(8,128)S(1)} %get-tuple-element.6) | data formatting | bytes 2097152 | tf_op jit(solution)/shard_map/mul | solution.py:55
  95.5 3.1 %fusion.4 = f32[2,256,512]{2,1,0:T(8,128)S(1)} fusion(bf16[2,256,256]{2,1,0:T(8,128)(2,1)S(1)} %bitcast.50, f32[512,2,256]{0,2,1:T(8,128)} %bitcast.51, f32[512,2,256]{0,2,1:T(8,128)} %bitcast.52, f32[2,256,512]{2,1,0:T(8,128)} %fusion.23, f32[]{:T(128)} %bitcast.10), kind=kOutput, calls=%fused_computation.12 | convolution fusion | flops 807403520 | bytes 4456452 | tf_op jit(solution)/shard_map/cbi,bki->cbk/dot_general | solution.py:58
  98.6 17.8 %all_to_all.30 = f32[512,8,64]{0,2,1:T(8,128)S(1)} all-to-all(f32[512,8,64]{0,2,1:T(8,128)S(1)} %bitcast.53), channel_id=1, replica_groups=mesh['fsdp'=8,'group'=4] {'fsdp'}, dimensions={1} | all-to-all | bytes 2097152 | tf_op jit(solution)/shard_map/all_to_all | solution.py:62
  116.4 1.6 %copy.35 = f32[8,512,1,64]{1,0,3,2:T(8,128)} copy(f32[8,512,1,64]{1,3,0,2:T(8,128)S(1)} %bitcast.45) | data formatting | bytes 2097152 | tf_op jit(solution)/shard_map/all_to_all | solution.py:62
  118.0 1.4 %reshape_squeeze.11 = f32[16,256,64]{1,0,2:T(8,128)S(1)} reshape(f32[8,512,1,64]{1,0,3,2:T(8,128)} %copy.35) | data formatting | bytes 2097152 | tf_op jit(solution)/shard_map/reshape;squeeze | solution.py:64
  119.4 2.3 %fusion.2 = bf16[64,16,256]{2,0,1:T(8,128)(2,1)S(1)} fusion(bf16[16,256,256]{2,1,0:T(8,128)(2,1)S(1)} %bitcast.42, f32[16,256,64]{1,0,2:T(8,128)S(1)} %reshape_squeeze.11), kind=kOutput, calls=%fused_computation.10 | convolution fusion | flops 805568512 | bytes 3670016 | tf_op jit(solution)/shard_map/blr,bjl->rbj/dot_general | solution.py:65
  121.7 0.3 copy.37
  122.0 1.0 convert_element_type.55
Async XLA Ops:
  7.2 48.1 %all-gather.3.cloned.1.call-start = ((), (), s32[]{:S(2)}) async-start(), calls=%async_computation.2 | async-start | bytes 2654208 | tf_op jit(solution)/shard_map/all_gather | solution.py:31
  59.0 1.4 %copy-start = (bf16[4608,256]{1,0:T(8,128)(2,1)}, bf16[4608,256]{1,0:T(8,128)(2,1)S(1)}, u32[]{:S(2)}) copy-start(bf16[4608,256]{1,0:T(8,128)(2,1)S(1)} %fusion) | copy-start | bytes 7077892
  65.1 19.2 %all-to-all-start = ((f32[64,8,512]{2,0,1:T(8,128)}), f32[64,8,512]{2,0,1:T(8,128)S(1)}, u32[]{:S(2)}, u32[]{:S(2)}) async-start(f32[64,8,512]{2,0,1:T(8,128)} %copy.31), calls=%async_computation | async-start | bytes 2097152 | tf_op jit(solution)/shard_map/all_to_all | solution.py:46
Sparse Core Ops, SparseCore 0:
  9.9 31.9 all-gather.2
where the time goes:
time: 131 us; the launch traced here: 130 us
  blocking collectives  60 us (46%)
  local copies, waits for them, and re-layouts  18.5 us (14%)
  between operations  16.2 us (12%)
  waiting for transfers between devices  15.1 us (12%)
  other arithmetic  8.67 us (7%)
  matrix products  7.53 us (6%)
  starting transfers between devices  3.82 us (3%)
    psum x1, blocking collectives, clip_of(): total = lax.psum(local_squares, ('fsdp', 'group'))  42.2 us
    all_to_all x1, blocking collectives, local(): lax.all_to_all(returning, 'fsdp', split_axis=1, concat_axis=0, tiled=True)  17.8 us
    all_to_all x1, waiting for transfers between devices, local(): lax.all_to_all(outgoing, 'fsdp', split_axis=1, concat_axis=0, tiled=True)  14.4 us
    reshape x2, local copies, waits for them, and re-layouts, local(): outgoing = turned.reshape(row_count, fsdp_count, col_share)  4.1 us
    all_to_all x1, starting transfers between devices, local(): lax.all_to_all(outgoing, 'fsdp', split_axis=1, concat_axis=0, tiled=True)  3.79 us
    concatenate x1, other arithmetic, local(): ordered_half = jnp.roll(gathered, -owner * owner_rows, axis=0)  3.73 us
    dot_general x1, matrix products, local(): jnp.einsum('cbi,bki->cbk', direction.reshape(col_share, left_blocks, BLOC...  3.12 us
    convert_element_type x1, other arithmetic, local(): second_sum[None].astype(jnp.bfloat16)  3.02 us
  transfers between devices with their start and end apart: 2, of which 1 were waited for; matrix products, arithmetic and copies ran while one was open for 3% of the time, Pallas kernels for 0%

commit v1 on v0

--- a/solution.py
+++ b/solution.py
@@ -11,8 +11,12 @@
 HIGHEST = lax.Precision.HIGHEST
 
 
+def create_streams(row_data):
+    return jax.lax.psum(jax.lax.psum(row_data, axis_name="group"), "fsdp")
+
+
 def clip_of(local_squares, entries):
-    total = lax.psum(local_squares, ("fsdp", "group"))
+    total = create_streams(local_squares)
     return jnp.float32(math.sqrt(entries)) / (jnp.sqrt(total) + 1e-06)
 
 

time: 131 us -> 117 us (0.89)
  blocking collectives: 60 us -> 44.4 us
  waiting for transfers between devices: 15.1 us -> 17.1 us
    psum x1 -> x2, blocking collectives: 42.2 us -> 26.6 us  [create_streams(): return jax.lax.psum(jax.lax.psum(row_data, axis_name='group'), 'fsdp')]
    all_gather x1, waiting for transfers between devices: 0.02 us -> 2.08 us  [local(): gathered = lax.all_gather(basis_store[0], 'fsdp', axis=0, tiled=True)]
  transfers between devices with their start and end apart: 2 -> 2, of which waited for: 1 -> 2; matrix products, arithmetic and copies ran while one was open for 3% -> 3% of each run, Pallas kernels for 0% -> 0%
where the time goes in v1:
time: 117 us; the launch traced here: 116 us
  blocking collectives  44.4 us (38%)
  local copies, waits for them, and re-layouts  18.6 us (16%)
  waiting for transfers between devices  17.1 us (15%)
  between operations  16.2 us (14%)
  other arithmetic  8.66 us (7%)
  matrix products  7.54 us (6%)
  starting transfers between devices  3.59 us (3%)
    psum x2, blocking collectives, create_streams(): return jax.lax.psum(jax.lax.psum(row_data, axis_name='group'), 'fsdp')  26.6 us
    all_to_all x1, blocking collectives, local(): lax.all_to_all(returning, 'fsdp', split_axis=1, concat_axis=0, tiled=True)  17.8 us
    all_to_all x1, waiting for transfers between devices, local(): lax.all_to_all(outgoing, 'fsdp', split_axis=1, concat_axis=0, tiled=True)  14.3 us
    reshape x2, local copies, waits for them, and re-layouts, local(): outgoing = turned.reshape(row_count, fsdp_count, col_share)  4.1 us
    concatenate x1, other arithmetic, local(): ordered_half = jnp.roll(gathered, -owner * owner_rows, axis=0)  3.71 us
    all_to_all x1, starting transfers between devices, local(): lax.all_to_all(outgoing, 'fsdp', split_axis=1, concat_axis=0, tiled=True)  3.56 us
    dot_general x1, matrix products, local(): jnp.einsum('cbi,bki->cbk', direction.reshape(col_share, left_blocks, BLOC...  3.11 us
    convert_element_type x1, other arithmetic, local(): second_sum[None].astype(jnp.bfloat16)  3.02 us
  transfers between devices with their start and end apart: 2, of which 2 were waited for; matrix products, arithmetic and copies ran while one was open for 3% of the time, Pallas kernels for 0%

profile of v1, /device:TPU:0, one launch (start us, length us, event | category | flops | bytes accessed | tf_op | source)
XLA Modules:
  0.0 116.0 jit_solution(82195408698684797)
XLA Ops:
  7.2 0.0 all-gather.3.cloned.1.call-start
  7.2 0.7 all-gather.3.cloned.1.call-update
  7.9 1.9 %multiply_reduce_fusion = f32[]{:T(128)} fusion(bf16[1,64,4096]{2,1,0:T(8,128)(2,1)} %param.6), kind=kLoop, calls=%fused_computation.24 | loop fusion | flops 786431 | bytes 524292 | tf_op jit(solution)/shard_map/reduce_sum | solution.py:34
  9.8 14.1 %psum.14 = f32[]{:T(128)} all-reduce(f32[]{:T(128)} %multiply_reduce_fusion), channel_id=1, replica_groups=mesh['fsdp'=8,'group'=4] {'group'}, use_global_device_ids=true, to_apply=%region_1.2 | all-reduce | flops 1 | bytes 8 | tf_op jit(solution)/shard_map/psum | solution.py:15
  23.9 12.6 %psum.15 = f32[]{:T(128)} all-reduce(f32[]{:T(128)} %psum.14), channel_id=1, replica_groups=mesh['fsdp'=8,'group'=4] {'fsdp'}, use_global_device_ids=true, to_apply=%region_2.3 | all-reduce | flops 1 | bytes 8 | tf_op jit(solution)/shard_map/psum | solution.py:15
  38.5 1.1 copy.42
  39.7 2.1 %all-gather.3.cloned.1.call-done = bf16[1,4608,256]{2,1,0:T(8,128)(2,1)} async-done(((bf16[1,576,256]{2,1,0:T(8,128)(2,1)}), bf16[1,4608,256]{2,1,0:T(8,128)(2,1)}) %all-gather.3.cloned.1.call-update) | async-done | bytes 2359312 | tf_op jit(solution)/shard_map/all_gather | solution.py:35
  41.8 3.7 %fusion = bf16[4608,256]{1,0:T(8,128)(2,1)S(1)} fusion(s32[]{:T(128)S(6)} %select_n.21, bf16[4608,256]{1,0:T(8,128)(2,1)} %bitcast.46), kind=kLoop, calls=%fused_computation.2 | loop fusion | flops 4718592 | bytes 4718596 | tf_op jit(solution)/shard_map/jit(_roll_dynamic)/concatenate | solution.py:38
  45.5 0.0 copy-start
  45.5 0.1 slice.8
  45.6 0.5 fusion.1
  46.1 0.8 copy-done
  46.9 0.6 copy.30
  47.5 1.3 %reshape.80 = f32[64,8,512]{2,1,0:T(8,128)} reshape(f32[64,16,256]{2,1,0:T(8,128)S(1)} %copy.30) | data formatting | bytes 2097152 | tf_op jit(solution)/shard_map/reshape | solution.py:49
  48.8 2.8 %copy.31 = f32[64,8,512]{2,0,1:T(8,128)} copy(f32[64,8,512]{2,1,0:T(8,128)} %reshape.80) | data formatting | bytes 2097152 | tf_op jit(solution)/shard_map/reshape | solution.py:49
  51.6 3.6 %all-to-all-start = ((f32[64,8,512]{2,0,1:T(8,128)}), f32[64,8,512]{2,0,1:T(8,128)S(1)}, u32[]{:S(2)}, u32[]{:S(2)}) async-start(f32[64,8,512]{2,0,1:T(8,128)} %copy.31), calls=%async_computation | async-start | bytes 2097152 | tf_op jit(solution)/shard_map/all_to_all | solution.py:50
  55.2 1.0 slice.9
  56.2 14.3 %all-to-all-done = f32[64,8,512]{2,0,1:T(8,128)S(1)} async-done(((f32[64,8,512]{2,0,1:T(8,128)}), f32[64,8,512]{2,0,1:T(8,128)S(1)}, u32[]{:S(2)}, u32[]{:S(2)}) %all-to-all-start) | async-done | bytes 1048608 | tf_op jit(solution)/shard_map/all_to_all | solution.py:50
  70.5 1.7 %fusion.23 = f32[2,256,512]{2,1,0:T(8,128)} fusion(bf16[2,256,256]{2,1,0:T(8,128)(2,1)S(1)} %bitcast.49, f32[2,256,512]{2,1,0:T(8,128)S(1)} %bitcast.43), kind=kOutput, calls=%fused_computation.32 | convolution fusion | flops 805306368 | bytes 2359296 | tf_op jit(solution)/shard_map/bkc,bki->cbi/dot_general | solution.py:53
  72.2 2.5 %copy.38 = f32[1,512,512]{2,1,0:T(8,128)} copy(f32[1,512,512]{1,2,0:T(8,128)} %bitcast.44) | data formatting | bytes 2097152 | tf_op jit(solution)/shard_map/reshape | solution.py:53
  74.7 3.0 %fusion.14 = (bf16[1,512,512]{2,1,0:T(8,128)(2,1)}, bf16[1,512,512]{2,1,0:T(8,128)(2,1)}, f32[1,512,512]{2,1,0:T(8,128)}, f32[1,512,512]{2,1,0:T(8,128)S(1)}) fusion(f32[1,512,512]{2,1,0:T(8,128)} %copy.38, bf16[1,512,512]{2,1,0:T(8,128)(2,1)} %param.8, bf16[1,512,512]{2,1,0:T(8,128)(2,1)} %param.7), kind=kLoop, calls=%fused_computation.20 | loop fusion | flops 2621440 | bytes 5242880 | tf_op jit(solution)/shard_map/convert_element_type | solution.py:73
  77.8 2.6 %copy.28 = f32[1,512,512]{1,2,0:T(8,128)} copy(f32[1,512,512]{2,1,0:T(8,128)} %get-tuple-element.5) | data formatting | bytes 2097152 | tf_op jit(solution)/shard_map/mul | solution.py:57
  80.4 1.3 %copy.33 = f32[1,512,512]{1,2,0:T(8,128)} copy(f32[1,512,512]{2,1,0:T(8,128)S(1)} %get-tuple-element.6) | data formatting | bytes 2097152 | tf_op jit(solution)/shard_map/mul | solution.py:59
  81.7 3.1 %fusion.4 = f32[2,256,512]{2,1,0:T(8,128)S(1)} fusion(bf16[2,256,256]{2,1,0:T(8,128)(2,1)S(1)} %bitcast.50, f32[512,2,256]{0,2,1:T(8,128)} %bitcast.51, f32[512,2,256]{0,2,1:T(8,128)} %bitcast.52, f32[2,256,512]{2,1,0:T(8,128)} %fusion.23, f32[]{:T(128)} %bitcast.10), kind=kOutput, calls=%fused_computation.12 | convolution fusion | flops 807403520 | bytes 4456452 | tf_op jit(solution)/shard_map/cbi,bki->cbk/dot_general | solution.py:62
  84.8 17.8 %all_to_all.30 = f32[512,8,64]{0,2,1:T(8,128)S(1)} all-to-all(f32[512,8,64]{0,2,1:T(8,128)S(1)} %bitcast.53), channel_id=1, replica_groups=mesh['fsdp'=8,'group'=4] {'fsdp'}, dimensions={1} | all-to-all | bytes 2097152 | tf_op jit(solution)/shard_map/all_to_all | solution.py:66
  102.6 1.6 %copy.35 = f32[8,512,1,64]{1,0,3,2:T(8,128)} copy(f32[8,512,1,64]{1,3,0,2:T(8,128)S(1)} %bitcast.45) | data formatting | bytes 2097152 | tf_op jit(solution)/shard_map/all_to_all | solution.py:66
  104.2 1.4 %reshape_squeeze.11 = f32[16,256,64]{1,0,2:T(8,128)S(1)} reshape(f32[8,512,1,64]{1,0,3,2:T(8,128)} %copy.35) | data formatting | bytes 2097152 | tf_op jit(solution)/shard_map/reshape;squeeze | solution.py:68
  105.6 2.3 %fusion.2 = bf16[64,16,256]{2,0,1:T(8,128)(2,1)S(1)} fusion(bf16[16,256,256]{2,1,0:T(8,128)(2,1)S(1)} %bitcast.42, f32[16,256,64]{1,0,2:T(8,128)S(1)} %reshape_squeeze.11), kind=kOutput, calls=%fused_computation.10 | convolution fusion | flops 805568512 | bytes 3670016 | tf_op jit(solution)/shard_map/blr,bjl->rbj/dot_general | solution.py:69
  107.9 0.3 copy.37
  108.2 1.0 convert_element_type.55
Async XLA Ops:
  7.2 34.6 %all-gather.3.cloned.1.call-start = ((), (), s32[]{:S(2)}) async-start(), calls=%async_computation.2 | async-start | bytes 2654208 | tf_op jit(solution)/shard_map/all_gather | solution.py:35
  45.5 1.4 %copy-start = (bf16[4608,256]{1,0:T(8,128)(2,1)}, bf16[4608,256]{1,0:T(8,128)(2,1)S(1)}, u32[]{:S(2)}) copy-start(bf16[4608,256]{1,0:T(8,128)(2,1)S(1)} %fusion) | copy-start | bytes 7077892
  51.6 18.9 %all-to-all-start = ((f32[64,8,512]{2,0,1:T(8,128)}), f32[64,8,512]{2,0,1:T(8,128)S(1)}, u32[]{:S(2)}, u32[]{:S(2)}) async-start(f32[64,8,512]{2,0,1:T(8,128)} %copy.31), calls=%async_computation | async-start | bytes 2097152 | tf_op jit(solution)/shard_map/all_to_all | solution.py:50
Sparse Core Ops, SparseCore 0:
  9.9 31.8 all-gather.2
